TPU v7x, 128 devices: a whole 4x4x4 slice. The times are simulated.
128 devices in a mesh: gx: 16 (over y, x), gy: 2 (over core), gz: 4 (over z).
Axes of the slice: x: 4, y: 4, z: 4, core: 2. Of those that a mesh axis runs over, the one named last changes fastest.
Arguments:
- density: float32 [384, 128, 512], P('gx', 'gy', 'gz'), may hold values from 0.8 to 1.25
- momentum: float32 [3, 384, 128, 512], P(None, 'gx', 'gy', 'gz'), may hold values from -1.5 to 1.5
- energy: float32 [384, 128, 512], P('gx', 'gy', 'gz'), may hold values from 2 to 3
- increment: float32 [5, 384, 128, 512], P(None, 'gx', 'gy', 'gz'), may hold values from -1.8 to 1.8
Outputs:
- new_state: float32 [5, 384, 128, 512], P(None, 'gx', 'gy', 'gz')
- new_increment: float32 [5, 384, 128, 512], P(None, 'gx', 'gy', 'gz')
All inputs are finite; a program needn't handle non-finite values.
Results may differ from a plain program's by a relative error of at most 0.0003.
Values sent between devices are 32-bit elements; how exact they have to be, the bound alone decides.
A program may use at most 128 MiB of HBM per device.

v0:
```python
import math

import jax
import jax.numpy as jnp
from jax import lax
from jax.sharding import PartitionSpec as P

deriv_alpha = 1.0 / 3.0
filter_alpha = 0.4999
gas_gamma = 1.4
time_step = 0.2
section_a = -5.0 / 9.0
section_b = 15.0 / 16.0
highest_precision = lax.Precision.HIGHEST


def from_behind(block, axis, distance):
    devices = range(lax.axis_size(axis))
    route = [((i - distance) % len(devices), i) for i in devices]
    return lax.ppermute(block, axis, route)


def padded_2(value, sides, width):
    for axis, dim in sides:
        size, length = (lax.axis_size(axis), value.shape[dim])
        up = [(i, (i + 1) % size) for i in range(size)]
        down = [(j, i) for i, j in up]
        last = lax.slice_in_dim(value, length - width, length, axis=dim)
        first = lax.slice_in_dim(value, 0, width, axis=dim)
        before = lax.ppermute(last, axis, up)
        after = lax.ppermute(first, axis, down)
        value = jnp.concatenate([before, value, after], axis=dim)
    return value


def root_of(coupling):
    return (-1.0 + math.sqrt(1.0 - 4.0 * coupling * coupling)) / (2.0 * coupling)


def signed_power(base_value, exponent):
    magnitude = jnp.power(jnp.float32(abs(base_value)), exponent.astype(jnp.float32))
    return jnp.where(exponent % 2 == 0, 1.0, -1.0).astype(jnp.float32) * magnitude


def filter_weights(coupling):
    return [
        (93.0 + 70.0 * coupling) / 128.0,
        (7.0 + 18.0 * coupling) / 16.0,
        (-7.0 + 14.0 * coupling) / 32.0,
        (1.0 - 2.0 * coupling) / 16.0,
        (-1.0 + 2.0 * coupling) / 128.0,
    ]


def fluxes(cell_block, axis_k):
    density = cell_block[0]
    momentum = cell_block[1:4]
    energy = cell_block[4]
    squared = momentum[0] * momentum[0] + momentum[1] * momentum[1] + momentum[2] * momentum[2]
    pressure = (gas_gamma - 1.0) * (energy - 0.5 * squared / density)
    velocity = momentum[axis_k] / density
    components = [
        momentum[axis_k],
        momentum[0] * velocity,
        momentum[1] * velocity,
        momentum[2] * velocity,
        (energy + pressure) * velocity,
    ]
    components[axis_k + 1] = components[axis_k + 1] + pressure
    return jnp.stack(components)


def stencil(field, along_axis, length):
    summed = None
    for offset, weight_n in ((1, 0.75), (2, -0.15), (3, 1.0 / 60.0)):
        upper_part = lax.slice_in_dim(field, 3 + offset, 3 + offset + length, axis=along_axis)
        lower_part = lax.slice_in_dim(field, 3 - offset, 3 - offset + length, axis=along_axis)
        term = weight_n * (upper_part - lower_part)
        summed = term if summed is None else summed + term
    return summed


def cycle_up(end_values, block_rate):

    def advance_cycle(index_loop, running):
        return from_behind(end_values + block_rate * running, "gx", 1)

    return lax.fori_loop(0, lax.axis_size("gx"), advance_cycle, jnp.zeros_like(end_values))


def cycle_down(end_values, block_rate):

    def advance_cycle(index_loop, running):
        return from_behind(end_values + block_rate * running, "gx", -1)

    return lax.fori_loop(0, lax.axis_size("gx"), advance_cycle, jnp.zeros_like(end_values))


def solve_lines(right_side, coupling):
    decay_rate = root_of(coupling)
    length = right_side.shape[1]
    block_rate = decay_rate**length
    closure = 1.0 - block_rate ** lax.axis_size("gx")
    row_index = jnp.arange(length, dtype=jnp.int32)
    offsets = row_index[:, None] - row_index[None, :]
    lower_table = jnp.where(offsets >= 0, signed_power(decay_rate, jnp.maximum(offsets, 0)), 0.0)
    forward = jnp.einsum("ij,vjyz->viyz", lower_table, right_side, precision=highest_precision)
    incoming = cycle_up(forward[:, length - 1], block_rate)
    forward = (
        forward
        + signed_power(decay_rate, row_index + 1)[None, :, None, None]
        * (incoming / closure)[:, None]
    )
    backward = jnp.einsum("ji,vjyz->viyz", lower_table, forward, precision=highest_precision)
    outgoing = cycle_down(backward[:, 0], block_rate)
    backward = (
        backward
        + signed_power(decay_rate, length - row_index)[None, :, None, None]
        * (outgoing / closure)[:, None]
    )
    return -(decay_rate / coupling) * backward


def on_device(density, momentum, energy, increment):
    fluid_state = jnp.concatenate([density[None], momentum, energy[None]], axis=0)
    x_cells = fluid_state.shape[1]
    wide_y = fluid_state.shape[2]
    wide_z = fluid_state.shape[3]
    padded = padded_2(fluid_state, (("gx", 1), ("gy", 2), ("gz", 3)), 3)
    flux_x = fluxes(padded[:, 1 : x_cells + 5, 3 : wide_y + 3, 3 : wide_z + 3], 0)
    compact_side = 7.0 / 9.0 * (
        flux_x[:, 3 : x_cells + 3] - flux_x[:, 1 : x_cells + 1]
    ) + 1.0 / 36.0 * (flux_x[:, 4 : x_cells + 4] - flux_x[:, 0:x_cells])
    flux_y = fluxes(padded[:, 3 : x_cells + 3, :, 3 : wide_z + 3], 1)
    flux_z = fluxes(padded[:, 3 : x_cells + 3, 3 : wide_y + 3, :], 2)
    side_terms = stencil(flux_y, 2, wide_y) + stencil(flux_z, 3, wide_z)
    spatial = solve_lines(compact_side, deriv_alpha) + side_terms
    new_increment = section_a * increment - time_step * spatial
    provisional = fluid_state + section_b * new_increment
    filter_pad = padded_2(provisional, (("gx", 1),), 4)
    weights = filter_weights(filter_alpha)
    filter_side = weights[0] * provisional
    for offset in range(1, 5):
        filter_side = filter_side + weights[offset] / 2.0 * (
            filter_pad[:, 4 + offset : x_cells + 4 + offset]
            + filter_pad[:, 4 - offset : x_cells + 4 - offset]
        )
    new_state = solve_lines(filter_side, filter_alpha)
    return (new_state, new_increment)


def solution(mesh):
    in_specs = (
        P("gx", "gy", "gz"),
        P(None, "gx", "gy", "gz"),
        P("gx", "gy", "gz"),
        P(None, "gx", "gy", "gz"),
    )
    out_specs = (P(None, "gx", "gy", "gz"), P(None, "gx", "gy", "gz"))
    return jax.shard_map(
        on_device, mesh=mesh, in_specs=in_specs, out_specs=out_specs, check_vma=False
    )
```

profile of v0, /device:TPU:0, one launch (start us, length us, event | category | flops | bytes accessed | tf_op | source)
XLA Modules:
  0.0 794.1 jit_solution(15469007991413552511)
XLA Ops:
  12.9 9.9 %collective-permute-done.5 = f32[5,3,64,128]{3,2,1,0:T(8,128)} collective-permute-done((f32[5,3,64,128]{3,2,1,0:T(8,128)}, f32[5,3,64,128]{3,2,1,0:T(8,128)}, u32[]{:S(2)}, u32[]{:S(2)}) %collective-permute-start.5) | collective-permute-done | bytes 491552 | tf_op jit(solution)/shard_map/ppermute | solution.py:31
  42.9 156.9 %while.40 = (s32[]{:T(128)}, f32[5,64,128]{2,1,0:T(8,128)S(1)}, f32[5,64,128]{2,1,0:T(8,128)S(1)}, s32[]{:T(128)}) while((s32[]{:T(128)}, f32[5,64,128]{2,1,0:T(8,128)S(1)}, f32[5,64,128]{2,1,0:T(8,128)S(1)}, s32[]{:T(128)}) %tuple.89), condition=%wide.region_1.2_spmd, body=%wide.region_0.1_spmd.sunk | while | flops 81922 | bytes 1146973 | solution.py:88
  43.8 9.7 %collective-permute-done = f32[5,64,128]{2,1,0:T(8,128)S(1)} collective-permute-done((f32[5,64,128]{2,1,0:T(8,128)}, f32[5,64,128]{2,1,0:T(8,128)S(1)}, u32[]{:S(2)}, u32[]{:S(2)}) %collective-permute-start) | collective-permute-done | bytes 163872 | tf_op jit(solution)/shard_map/while/body/eval_jaxpr/ppermute | solution.py:20
  54.2 8.9 %collective-permute-done = f32[5,64,128]{2,1,0:T(8,128)S(1)} collective-permute-done((f32[5,64,128]{2,1,0:T(8,128)}, f32[5,64,128]{2,1,0:T(8,128)S(1)}, u32[]{:S(2)}, u32[]{:S(2)}) %collective-permute-start) | collective-permute-done | bytes 163872 | tf_op jit(solution)/shard_map/while/body/eval_jaxpr/ppermute | solution.py:20
  63.8 8.8 %collective-permute-done = f32[5,64,128]{2,1,0:T(8,128)S(1)} collective-permute-done((f32[5,64,128]{2,1,0:T(8,128)}, f32[5,64,128]{2,1,0:T(8,128)S(1)}, u32[]{:S(2)}, u32[]{:S(2)}) %collective-permute-start) | collective-permute-done | bytes 163872 | tf_op jit(solution)/shard_map/while/body/eval_jaxpr/ppermute | solution.py:20
  73.3 8.8 %collective-permute-done = f32[5,64,128]{2,1,0:T(8,128)S(1)} collective-permute-done((f32[5,64,128]{2,1,0:T(8,128)}, f32[5,64,128]{2,1,0:T(8,128)S(1)}, u32[]{:S(2)}, u32[]{:S(2)}) %collective-permute-start) | collective-permute-done | bytes 163872 | tf_op jit(solution)/shard_map/while/body/eval_jaxpr/ppermute | solution.py:20
  82.9 8.8 %collective-permute-done = f32[5,64,128]{2,1,0:T(8,128)S(1)} collective-permute-done((f32[5,64,128]{2,1,0:T(8,128)}, f32[5,64,128]{2,1,0:T(8,128)S(1)}, u32[]{:S(2)}, u32[]{:S(2)}) %collective-permute-start) | collective-permute-done | bytes 163872 | tf_op jit(solution)/shard_map/while/body/eval_jaxpr/ppermute | solution.py:20
  92.4 8.8 %collective-permute-done = f32[5,64,128]{2,1,0:T(8,128)S(1)} collective-permute-done((f32[5,64,128]{2,1,0:T(8,128)}, f32[5,64,128]{2,1,0:T(8,128)S(1)}, u32[]{:S(2)}, u32[]{:S(2)}) %collective-permute-start) | collective-permute-done | bytes 163872 | tf_op jit(solution)/shard_map/while/body/eval_jaxpr/ppermute | solution.py:20
  101.9 9.4 %collective-permute-done = f32[5,64,128]{2,1,0:T(8,128)S(1)} collective-permute-done((f32[5,64,128]{2,1,0:T(8,128)}, f32[5,64,128]{2,1,0:T(8,128)S(1)}, u32[]{:S(2)}, u32[]{:S(2)}) %collective-permute-start) | collective-permute-done | bytes 163872 | tf_op jit(solution)/shard_map/while/body/eval_jaxpr/ppermute | solution.py:20
  112.0 10.5 %collective-permute-done = f32[5,64,128]{2,1,0:T(8,128)S(1)} collective-permute-done((f32[5,64,128]{2,1,0:T(8,128)}, f32[5,64,128]{2,1,0:T(8,128)S(1)}, u32[]{:S(2)}, u32[]{:S(2)}) %collective-permute-start) | collective-permute-done | bytes 163872 | tf_op jit(solution)/shard_map/while/body/eval_jaxpr/ppermute | solution.py:20
  123.2 9.7 %collective-permute-done = f32[5,64,128]{2,1,0:T(8,128)S(1)} collective-permute-done((f32[5,64,128]{2,1,0:T(8,128)}, f32[5,64,128]{2,1,0:T(8,128)S(1)}, u32[]{:S(2)}, u32[]{:S(2)}) %collective-permute-start) | collective-permute-done | bytes 163872 | tf_op jit(solution)/shard_map/while/body/eval_jaxpr/ppermute | solution.py:20
  133.6 8.9 %collective-permute-done = f32[5,64,128]{2,1,0:T(8,128)S(1)} collective-permute-done((f32[5,64,128]{2,1,0:T(8,128)}, f32[5,64,128]{2,1,0:T(8,128)S(1)}, u32[]{:S(2)}, u32[]{:S(2)}) %collective-permute-start) | collective-permute-done | bytes 163872 | tf_op jit(solution)/shard_map/while/body/eval_jaxpr/ppermute | solution.py:20
  143.2 8.8 %collective-permute-done = f32[5,64,128]{2,1,0:T(8,128)S(1)} collective-permute-done((f32[5,64,128]{2,1,0:T(8,128)}, f32[5,64,128]{2,1,0:T(8,128)S(1)}, u32[]{:S(2)}, u32[]{:S(2)}) %collective-permute-start) | collective-permute-done | bytes 163872 | tf_op jit(solution)/shard_map/while/body/eval_jaxpr/ppermute | solution.py:20
  152.7 8.8 %collective-permute-done = f32[5,64,128]{2,1,0:T(8,128)S(1)} collective-permute-done((f32[5,64,128]{2,1,0:T(8,128)}, f32[5,64,128]{2,1,0:T(8,128)S(1)}, u32[]{:S(2)}, u32[]{:S(2)}) %collective-permute-start) | collective-permute-done | bytes 163872 | tf_op jit(solution)/shard_map/while/body/eval_jaxpr/ppermute | solution.py:20
  162.3 8.8 %collective-permute-done = f32[5,64,128]{2,1,0:T(8,128)S(1)} collective-permute-done((f32[5,64,128]{2,1,0:T(8,128)}, f32[5,64,128]{2,1,0:T(8,128)S(1)}, u32[]{:S(2)}, u32[]{:S(2)}) %collective-permute-start) | collective-permute-done | bytes 163872 | tf_op jit(solution)/shard_map/while/body/eval_jaxpr/ppermute | solution.py:20
  171.8 8.8 %collective-permute-done = f32[5,64,128]{2,1,0:T(8,128)S(1)} collective-permute-done((f32[5,64,128]{2,1,0:T(8,128)}, f32[5,64,128]{2,1,0:T(8,128)S(1)}, u32[]{:S(2)}, u32[]{:S(2)}) %collective-permute-start) | collective-permute-done | bytes 163872 | tf_op jit(solution)/shard_map/while/body/eval_jaxpr/ppermute | solution.py:20
  181.3 8.8 %collective-permute-done = f32[5,64,128]{2,1,0:T(8,128)S(1)} collective-permute-done((f32[5,64,128]{2,1,0:T(8,128)}, f32[5,64,128]{2,1,0:T(8,128)S(1)}, u32[]{:S(2)}, u32[]{:S(2)}) %collective-permute-start) | collective-permute-done | bytes 163872 | tf_op jit(solution)/shard_map/while/body/eval_jaxpr/ppermute | solution.py:20
  190.9 8.8 %collective-permute-done = f32[5,64,128]{2,1,0:T(8,128)S(1)} collective-permute-done((f32[5,64,128]{2,1,0:T(8,128)}, f32[5,64,128]{2,1,0:T(8,128)S(1)}, u32[]{:S(2)}, u32[]{:S(2)}) %collective-permute-start) | collective-permute-done | bytes 163872 | tf_op jit(solution)/shard_map/while/body/eval_jaxpr/ppermute | solution.py:20
  254.4 16.3 %pad_maximum_fusion = f32[5,30,70,134]{3,1,2,0:T(8,128)S(1)} fusion(f32[5,30,70,3]{3,1,2,0:T(8,128)} %copy.26, f32[5,30,3,128]{3,1,2,0:T(8,128)} %collective-permute-done.7, f32[5,3,64,128]{3,1,2,0:T(4,128)} %copy-done.6, f32[1,24,64,128]{3,1,2,0:T(8,128)S(1)} %get-tuple-element.123, f32[3,24,64,128]{3,1,2,0:T(8,128)S(1)} %copy.16, ...), kind=kLoop, calls=%fused_computation.4 | loop fusion | flops 11256000 | bytes 11256000 | tf_op jit(solution)/shard_map/concatenate | solution.py:32
  279.5 150.5 %while.41 = (s32[]{:T(128)}, f32[5,64,128]{2,1,0:T(8,128)S(1)}, f32[5,64,128]{2,1,0:T(8,128)S(1)}, s32[]{:T(128)}) while((s32[]{:T(128)}, f32[5,64,128]{2,1,0:T(8,128)S(1)}, f32[5,64,128]{2,1,0:T(8,128)S(1)}, s32[]{:T(128)}) %tuple.87), condition=%wide.region_3.4_spmd, body=%wide.region_2.3_spmd.sunk | while | flops 81922 | bytes 1146973 | solution.py:96
  429.9 29.2 %multiply_add_fusion.4 = (f32[5,24,64,128]{3,1,2,0:T(8,128)}, f32[5,24,64,128]{3,1,2,0:T(8,128)}) fusion(f32[1,24,64,128]{3,1,2,0:T(8,128)S(1)} %get-tuple-element.123, f32[3,24,64,128]{3,1,2,0:T(8,128)S(1)} %copy.16, f32[1,24,64,128]{3,1,2,0:T(8,128)} %copy-done.1, f32[5,24,64,134]{3,1,2,0:T(8,128)} %multiply_dynamic-update-slice_fusion, ...), kind=kLoop, calls=%fused_computation.77 | loop fusion | flops 27525120 | bytes 67010656 | tf_op jit(solution)/shard_map/add | solution.py:139
  476.5 19.1 %fusion.66 = f32[5,24,64,128]{3,1,2,0:T(8,128)} fusion(f32[5,24,64,128]{3,1,2,0:T(8,128)} %get-tuple-element.102, f32[5,4,64,128]{3,1,2,0:T(4,128)S(1)} %collective-permute-done.11, f32[5,4,64,128]{3,1,2,0:T(4,128)S(1)} %collective-permute-done.10), kind=kOutput, calls=%fused_computation.84 | convolution fusion | flops 303767424 | bytes 9175040 | tf_op jit(solution)/shard_map/ij,vjyz->viyz/dot_general | solution.py:107
  497.1 145.1 %while.42 = (s32[]{:T(128)}, f32[5,64,128]{2,1,0:T(8,128)S(1)}, f32[5,64,128]{2,1,0:T(8,128)S(1)}, s32[]{:T(128)}) while((s32[]{:T(128)}, f32[5,64,128]{2,1,0:T(8,128)S(1)}, f32[5,64,128]{2,1,0:T(8,128)S(1)}, s32[]{:T(128)}) %tuple.90), condition=%wide.region_5.6_spmd, body=%wide.region_4.5_spmd.sunk | while | flops 81922 | bytes 1146973 | solution.py:88
  497.2 8.6 %collective-permute-done.2 = f32[5,64,128]{2,1,0:T(8,128)S(1)} collective-permute-done((f32[5,64,128]{2,1,0:T(8,128)S(1)}, f32[5,64,128]{2,1,0:T(8,128)S(1)}, u32[]{:S(2)}, u32[]{:S(2)}) %collective-permute-start.2) | collective-permute-done | bytes 163872 | tf_op jit(solution)/shard_map/while/body/eval_jaxpr/ppermute | solution.py:20
  506.0 9.5 %collective-permute-done.2 = f32[5,64,128]{2,1,0:T(8,128)S(1)} collective-permute-done((f32[5,64,128]{2,1,0:T(8,128)S(1)}, f32[5,64,128]{2,1,0:T(8,128)S(1)}, u32[]{:S(2)}, u32[]{:S(2)}) %collective-permute-start.2) | collective-permute-done | bytes 163872 | tf_op jit(solution)/shard_map/while/body/eval_jaxpr/ppermute | solution.py:20
  515.5 10.1 %collective-permute-done.2 = f32[5,64,128]{2,1,0:T(8,128)S(1)} collective-permute-done((f32[5,64,128]{2,1,0:T(8,128)S(1)}, f32[5,64,128]{2,1,0:T(8,128)S(1)}, u32[]{:S(2)}, u32[]{:S(2)}) %collective-permute-start.2) | collective-permute-done | bytes 163872 | tf_op jit(solution)/shard_map/while/body/eval_jaxpr/ppermute | solution.py:20
  525.8 9.3 %collective-permute-done.2 = f32[5,64,128]{2,1,0:T(8,128)S(1)} collective-permute-done((f32[5,64,128]{2,1,0:T(8,128)S(1)}, f32[5,64,128]{2,1,0:T(8,128)S(1)}, u32[]{:S(2)}, u32[]{:S(2)}) %collective-permute-start.2) | collective-permute-done | bytes 163872 | tf_op jit(solution)/shard_map/while/body/eval_jaxpr/ppermute | solution.py:20
  535.2 8.6 %collective-permute-done.2 = f32[5,64,128]{2,1,0:T(8,128)S(1)} collective-permute-done((f32[5,64,128]{2,1,0:T(8,128)S(1)}, f32[5,64,128]{2,1,0:T(8,128)S(1)}, u32[]{:S(2)}, u32[]{:S(2)}) %collective-permute-start.2) | collective-permute-done | bytes 163872 | tf_op jit(solution)/shard_map/while/body/eval_jaxpr/ppermute | solution.py:20
  543.9 8.6 %collective-permute-done.2 = f32[5,64,128]{2,1,0:T(8,128)S(1)} collective-permute-done((f32[5,64,128]{2,1,0:T(8,128)S(1)}, f32[5,64,128]{2,1,0:T(8,128)S(1)}, u32[]{:S(2)}, u32[]{:S(2)}) %collective-permute-start.2) | collective-permute-done | bytes 163872 | tf_op jit(solution)/shard_map/while/body/eval_jaxpr/ppermute | solution.py:20
  570.1 9.3 %collective-permute-done.2 = f32[5,64,128]{2,1,0:T(8,128)S(1)} collective-permute-done((f32[5,64,128]{2,1,0:T(8,128)S(1)}, f32[5,64,128]{2,1,0:T(8,128)S(1)}, u32[]{:S(2)}, u32[]{:S(2)}) %collective-permute-start.2) | collective-permute-done | bytes 163872 | tf_op jit(solution)/shard_map/while/body/eval_jaxpr/ppermute | solution.py:20
  579.6 10.3 %collective-permute-done.2 = f32[5,64,128]{2,1,0:T(8,128)S(1)} collective-permute-done((f32[5,64,128]{2,1,0:T(8,128)S(1)}, f32[5,64,128]{2,1,0:T(8,128)S(1)}, u32[]{:S(2)}, u32[]{:S(2)}) %collective-permute-start.2) | collective-permute-done | bytes 163872 | tf_op jit(solution)/shard_map/while/body/eval_jaxpr/ppermute | solution.py:20
  650.4 138.2 %while.43 = (s32[]{:T(128)}, f32[5,64,128]{2,1,0:T(8,128)S(1)}, f32[5,64,128]{2,1,0:T(8,128)S(1)}, s32[]{:T(128)}) while((s32[]{:T(128)}, f32[5,64,128]{2,1,0:T(8,128)S(1)}, f32[5,64,128]{2,1,0:T(8,128)S(1)}, s32[]{:T(128)}) %tuple.88), condition=%wide.region_7.8_spmd, body=%wide.region_6.7_spmd.sunk | while | flops 81922 | bytes 1146973 | solution.py:96
  (261 shorter events, 497.8 us)
Async XLA Ops:
  6.7 16.1 %collective-permute-start.5 = (f32[5,3,64,128]{3,2,1,0:T(8,128)}, f32[5,3,64,128]{3,2,1,0:T(8,128)}, u32[]{:S(2)}, u32[]{:S(2)}) collective-permute-start(f32[5,3,64,128]{3,2,1,0:T(8,128)} %copy.19), channel_id=1, source_target_pairs={{8,0},{16,8},{24,16},{32,24},{40,32},{48,40},{56,48},{64,56},{72,6... | collective-permute-start | bytes 1474568 | tf_op jit(solution)/shard_map/ppermute | solution.py:31
  12.9 16.3 %collective-permute-start.4 = (f32[5,3,64,128]{3,2,1,0:T(8,128)}, f32[5,3,64,128]{3,2,1,0:T(8,128)}, u32[]{:S(2)}, u32[]{:S(2)}) collective-permute-start(f32[5,3,64,128]{3,2,1,0:T(8,128)} %copy.18), channel_id=1, source_target_pairs={{0,8},{8,16},{16,24},{24,32},{32,40},{40,48},{48,56},{56,64},{64,7... | collective-permute-start | bytes 1474568 | tf_op jit(solution)/shard_map/ppermute | solution.py:30
  33.5 172.6 %collective-permute-start.7 = (f32[5,30,3,128]{3,1,2,0:T(8,128)}, f32[5,30,3,128]{3,1,2,0:T(8,128)}, u32[]{:S(2)}, u32[]{:S(2)}) collective-permute-start(f32[5,30,3,128]{3,1,2,0:T(8,128)} %get-tuple-element.118), channel_id=1, source_target_pairs={{4,0},{0,4},{5,1},{1,5},{6,2},{2,6},{7,3},{3,7},{12,8},{8,12},{13,... | collective-permute-start | bytes 691208 | tf_op jit(solution)/shard_map/ppermute | solution.py:31
  33.6 174.3 %collective-permute-start.6 = (f32[5,30,3,128]{3,1,2,0:T(8,128)}, f32[5,30,3,128]{3,1,2,0:T(8,128)}, u32[]{:S(2)}, u32[]{:S(2)}) collective-permute-start(f32[5,30,3,128]{3,1,2,0:T(8,128)} %get-tuple-element.117), channel_id=1, source_target_pairs={{0,4},{4,0},{1,5},{5,1},{2,6},{6,2},{3,7},{7,3},{8,12},{12,8},{9,1... | collective-permute-start | bytes 691208 | tf_op jit(solution)/shard_map/ppermute | solution.py:30
  43.8 9.8 %collective-permute-start = (f32[5,64,128]{2,1,0:T(8,128)}, f32[5,64,128]{2,1,0:T(8,128)S(1)}, u32[]{:S(2)}, u32[]{:S(2)}) collective-permute-start(f32[5,64,128]{2,1,0:T(8,128)} %multiply_add_fusion.9), channel_id=1, source_target_pairs={{120,0},{0,8},{8,16},{16,24},{24,32},{32,40},{40,48},{48,56},{56,6... | collective-permute-start | bytes 491528 | tf_op jit(solution)/shard_map/while/body/eval_jaxpr/ppermute | solution.py:20
  54.2 8.9 %collective-permute-start = (f32[5,64,128]{2,1,0:T(8,128)}, f32[5,64,128]{2,1,0:T(8,128)S(1)}, u32[]{:S(2)}, u32[]{:S(2)}) collective-permute-start(f32[5,64,128]{2,1,0:T(8,128)} %multiply_add_fusion.9), channel_id=1, source_target_pairs={{120,0},{0,8},{8,16},{16,24},{24,32},{32,40},{40,48},{48,56},{56,6... | collective-permute-start | bytes 491528 | tf_op jit(solution)/shard_map/while/body/eval_jaxpr/ppermute | solution.py:20
  101.9 9.4 %collective-permute-start = (f32[5,64,128]{2,1,0:T(8,128)}, f32[5,64,128]{2,1,0:T(8,128)S(1)}, u32[]{:S(2)}, u32[]{:S(2)}) collective-permute-start(f32[5,64,128]{2,1,0:T(8,128)} %multiply_add_fusion.9), channel_id=1, source_target_pairs={{120,0},{0,8},{8,16},{16,24},{24,32},{32,40},{40,48},{48,56},{56,6... | collective-permute-start | bytes 491528 | tf_op jit(solution)/shard_map/while/body/eval_jaxpr/ppermute | solution.py:20
  112.0 10.5 %collective-permute-start = (f32[5,64,128]{2,1,0:T(8,128)}, f32[5,64,128]{2,1,0:T(8,128)S(1)}, u32[]{:S(2)}, u32[]{:S(2)}) collective-permute-start(f32[5,64,128]{2,1,0:T(8,128)} %multiply_add_fusion.9), channel_id=1, source_target_pairs={{120,0},{0,8},{8,16},{16,24},{24,32},{32,40},{40,48},{48,56},{56,6... | collective-permute-start | bytes 491528 | tf_op jit(solution)/shard_map/while/body/eval_jaxpr/ppermute | solution.py:20
  123.2 9.8 %collective-permute-start = (f32[5,64,128]{2,1,0:T(8,128)}, f32[5,64,128]{2,1,0:T(8,128)S(1)}, u32[]{:S(2)}, u32[]{:S(2)}) collective-permute-start(f32[5,64,128]{2,1,0:T(8,128)} %multiply_add_fusion.9), channel_id=1, source_target_pairs={{120,0},{0,8},{8,16},{16,24},{24,32},{32,40},{40,48},{48,56},{56,6... | collective-permute-start | bytes 491528 | tf_op jit(solution)/shard_map/while/body/eval_jaxpr/ppermute | solution.py:20
  133.6 8.9 %collective-permute-start = (f32[5,64,128]{2,1,0:T(8,128)}, f32[5,64,128]{2,1,0:T(8,128)S(1)}, u32[]{:S(2)}, u32[]{:S(2)}) collective-permute-start(f32[5,64,128]{2,1,0:T(8,128)} %multiply_add_fusion.9), channel_id=1, source_target_pairs={{120,0},{0,8},{8,16},{16,24},{24,32},{32,40},{40,48},{48,56},{56,6... | collective-permute-start | bytes 491528 | tf_op jit(solution)/shard_map/while/body/eval_jaxpr/ppermute | solution.py:20
  223.3 20.9 %collective-permute-start.9 = (f32[5,30,70,3]{2,1,3,0:T(8,128)}, f32[5,30,70,3]{2,1,3,0:T(8,128)}, u32[]{:S(2)}, u32[]{:S(2)}) collective-permute-start(f32[5,30,70,3]{2,1,3,0:T(8,128)} %copy.24), channel_id=1, source_target_pairs={{1,0},{2,1},{3,2},{0,3},{5,4},{6,5},{7,6},{4,7},{9,8},{10,9},{11,1... | collective-permute-start | bytes 378008 | tf_op jit(solution)/shard_map/ppermute | solution.py:31
  232.1 17.4 %collective-permute-start.8 = (f32[5,30,70,3]{2,1,3,0:T(8,128)}, f32[5,30,70,3]{2,1,3,0:T(8,128)}, u32[]{:S(2)}, u32[]{:S(2)}) collective-permute-start(f32[5,30,70,3]{2,1,3,0:T(8,128)} %copy.23), channel_id=1, source_target_pairs={{0,1},{1,2},{2,3},{3,0},{4,5},{5,6},{6,7},{7,4},{8,9},{9,10},{10,1... | collective-permute-start | bytes 378008 | tf_op jit(solution)/shard_map/ppermute | solution.py:30
  294.2 8.8 %collective-permute-start.1 = (f32[5,64,128]{2,1,0:T(8,128)}, f32[5,64,128]{2,1,0:T(8,128)S(1)}, u32[]{:S(2)}, u32[]{:S(2)}) collective-permute-start(f32[5,64,128]{2,1,0:T(8,128)} %multiply_add_fusion.10), channel_id=1, source_target_pairs={{8,0},{16,8},{24,16},{32,24},{40,32},{48,40},{56,48},{64,56},{72,6... | collective-permute-start | bytes 491528 | tf_op jit(solution)/shard_map/while/body/eval_jaxpr/ppermute | solution.py:20
  303.8 8.8 %collective-permute-start.1 = (f32[5,64,128]{2,1,0:T(8,128)}, f32[5,64,128]{2,1,0:T(8,128)S(1)}, u32[]{:S(2)}, u32[]{:S(2)}) collective-permute-start(f32[5,64,128]{2,1,0:T(8,128)} %multiply_add_fusion.10), channel_id=1, source_target_pairs={{8,0},{16,8},{24,16},{32,24},{40,32},{48,40},{56,48},{64,56},{72,6... | collective-permute-start | bytes 491528 | tf_op jit(solution)/shard_map/while/body/eval_jaxpr/ppermute | solution.py:20
  313.3 8.8 %collective-permute-start.1 = (f32[5,64,128]{2,1,0:T(8,128)}, f32[5,64,128]{2,1,0:T(8,128)S(1)}, u32[]{:S(2)}, u32[]{:S(2)}) collective-permute-start(f32[5,64,128]{2,1,0:T(8,128)} %multiply_add_fusion.10), channel_id=1, source_target_pairs={{8,0},{16,8},{24,16},{32,24},{40,32},{48,40},{56,48},{64,56},{72,6... | collective-permute-start | bytes 491528 | tf_op jit(solution)/shard_map/while/body/eval_jaxpr/ppermute | solution.py:20
  322.8 8.8 %collective-permute-start.1 = (f32[5,64,128]{2,1,0:T(8,128)}, f32[5,64,128]{2,1,0:T(8,128)S(1)}, u32[]{:S(2)}, u32[]{:S(2)}) collective-permute-start(f32[5,64,128]{2,1,0:T(8,128)} %multiply_add_fusion.10), channel_id=1, source_target_pairs={{8,0},{16,8},{24,16},{32,24},{40,32},{48,40},{56,48},{64,56},{72,6... | collective-permute-start | bytes 491528 | tf_op jit(solution)/shard_map/while/body/eval_jaxpr/ppermute | solution.py:20
  332.4 9.9 %collective-permute-start.1 = (f32[5,64,128]{2,1,0:T(8,128)}, f32[5,64,128]{2,1,0:T(8,128)S(1)}, u32[]{:S(2)}, u32[]{:S(2)}) collective-permute-start(f32[5,64,128]{2,1,0:T(8,128)} %multiply_add_fusion.10), channel_id=1, source_target_pairs={{8,0},{16,8},{24,16},{32,24},{40,32},{48,40},{56,48},{64,56},{72,6... | collective-permute-start | bytes 491528 | tf_op jit(solution)/shard_map/while/body/eval_jaxpr/ppermute | solution.py:20
  343.0 10.2 %collective-permute-start.1 = (f32[5,64,128]{2,1,0:T(8,128)}, f32[5,64,128]{2,1,0:T(8,128)S(1)}, u32[]{:S(2)}, u32[]{:S(2)}) collective-permute-start(f32[5,64,128]{2,1,0:T(8,128)} %multiply_add_fusion.10), channel_id=1, source_target_pairs={{8,0},{16,8},{24,16},{32,24},{40,32},{48,40},{56,48},{64,56},{72,6... | collective-permute-start | bytes 491528 | tf_op jit(solution)/shard_map/while/body/eval_jaxpr/ppermute | solution.py:20
  353.8 9.3 %collective-permute-start.1 = (f32[5,64,128]{2,1,0:T(8,128)}, f32[5,64,128]{2,1,0:T(8,128)S(1)}, u32[]{:S(2)}, u32[]{:S(2)}) collective-permute-start(f32[5,64,128]{2,1,0:T(8,128)} %multiply_add_fusion.10), channel_id=1, source_target_pairs={{8,0},{16,8},{24,16},{32,24},{40,32},{48,40},{56,48},{64,56},{72,6... | collective-permute-start | bytes 491528 | tf_op jit(solution)/shard_map/while/body/eval_jaxpr/ppermute | solution.py:20
  363.8 8.8 %collective-permute-start.1 = (f32[5,64,128]{2,1,0:T(8,128)}, f32[5,64,128]{2,1,0:T(8,128)S(1)}, u32[]{:S(2)}, u32[]{:S(2)}) collective-permute-start(f32[5,64,128]{2,1,0:T(8,128)} %multiply_add_fusion.10), channel_id=1, source_target_pairs={{8,0},{16,8},{24,16},{32,24},{40,32},{48,40},{56,48},{64,56},{72,6... | collective-permute-start | bytes 491528 | tf_op jit(solution)/shard_map/while/body/eval_jaxpr/ppermute | solution.py:20
  373.4 8.8 %collective-permute-start.1 = (f32[5,64,128]{2,1,0:T(8,128)}, f32[5,64,128]{2,1,0:T(8,128)S(1)}, u32[]{:S(2)}, u32[]{:S(2)}) collective-permute-start(f32[5,64,128]{2,1,0:T(8,128)} %multiply_add_fusion.10), channel_id=1, source_target_pairs={{8,0},{16,8},{24,16},{32,24},{40,32},{48,40},{56,48},{64,56},{72,6... | collective-permute-start | bytes 491528 | tf_op jit(solution)/shard_map/while/body/eval_jaxpr/ppermute | solution.py:20
  382.9 8.8 %collective-permute-start.1 = (f32[5,64,128]{2,1,0:T(8,128)}, f32[5,64,128]{2,1,0:T(8,128)S(1)}, u32[]{:S(2)}, u32[]{:S(2)}) collective-permute-start(f32[5,64,128]{2,1,0:T(8,128)} %multiply_add_fusion.10), channel_id=1, source_target_pairs={{8,0},{16,8},{24,16},{32,24},{40,32},{48,40},{56,48},{64,56},{72,6... | collective-permute-start | bytes 491528 | tf_op jit(solution)/shard_map/while/body/eval_jaxpr/ppermute | solution.py:20
  461.1 15.4 %collective-permute-start.11 = (f32[5,4,64,128]{3,1,2,0:T(4,128)S(1)}, f32[5,4,64,128]{3,1,2,0:T(4,128)S(1)}, u32[]{:S(2)}, u32[]{:S(2)}) collective-permute-start(f32[5,4,64,128]{3,1,2,0:T(4,128)S(1)} %get-tuple-element.120), channel_id=1, source_target_pairs={{0,8},{8,16},{16,24},{24,32},{32,40},{40,48},{48,56},{56,64},{64,7... | collective-permute-start | bytes 1966088 | tf_op jit(solution)/shard_map/ppermute | solution.py:30
  461.4 15.1 %collective-permute-start.10 = (f32[5,4,64,128]{3,1,2,0:T(4,128)S(1)}, f32[5,4,64,128]{3,1,2,0:T(4,128)S(1)}, u32[]{:S(2)}, u32[]{:S(2)}) collective-permute-start(f32[5,4,64,128]{3,1,2,0:T(4,128)S(1)} %get-tuple-element.119), channel_id=1, source_target_pairs={{8,0},{16,8},{24,16},{32,24},{40,32},{48,40},{56,48},{64,56},{72,6... | collective-permute-start | bytes 1966088 | tf_op jit(solution)/shard_map/ppermute | solution.py:31
  505.9 9.5 %collective-permute-start.2 = (f32[5,64,128]{2,1,0:T(8,128)S(1)}, f32[5,64,128]{2,1,0:T(8,128)S(1)}, u32[]{:S(2)}, u32[]{:S(2)}) collective-permute-start(f32[5,64,128]{2,1,0:T(8,128)S(1)} %multiply_add_fusion.11), channel_id=1, source_target_pairs={{120,0},{0,8},{8,16},{16,24},{24,32},{32,40},{40,48},{48,56},{56,6... | collective-permute-start | bytes 491528 | tf_op jit(solution)/shard_map/while/body/eval_jaxpr/ppermute | solution.py:20
  515.4 10.2 %collective-permute-start.2 = (f32[5,64,128]{2,1,0:T(8,128)S(1)}, f32[5,64,128]{2,1,0:T(8,128)S(1)}, u32[]{:S(2)}, u32[]{:S(2)}) collective-permute-start(f32[5,64,128]{2,1,0:T(8,128)S(1)} %multiply_add_fusion.11), channel_id=1, source_target_pairs={{120,0},{0,8},{8,16},{16,24},{24,32},{32,40},{40,48},{48,56},{56,6... | collective-permute-start | bytes 491528 | tf_op jit(solution)/shard_map/while/body/eval_jaxpr/ppermute | solution.py:20
  525.7 9.4 %collective-permute-start.2 = (f32[5,64,128]{2,1,0:T(8,128)S(1)}, f32[5,64,128]{2,1,0:T(8,128)S(1)}, u32[]{:S(2)}, u32[]{:S(2)}) collective-permute-start(f32[5,64,128]{2,1,0:T(8,128)S(1)} %multiply_add_fusion.11), channel_id=1, source_target_pairs={{120,0},{0,8},{8,16},{16,24},{24,32},{32,40},{40,48},{48,56},{56,6... | collective-permute-start | bytes 491528 | tf_op jit(solution)/shard_map/while/body/eval_jaxpr/ppermute | solution.py:20
  570.0 9.4 %collective-permute-start.2 = (f32[5,64,128]{2,1,0:T(8,128)S(1)}, f32[5,64,128]{2,1,0:T(8,128)S(1)}, u32[]{:S(2)}, u32[]{:S(2)}) collective-permute-start(f32[5,64,128]{2,1,0:T(8,128)S(1)} %multiply_add_fusion.11), channel_id=1, source_target_pairs={{120,0},{0,8},{8,16},{16,24},{24,32},{32,40},{40,48},{48,56},{56,6... | collective-permute-start | bytes 491528 | tf_op jit(solution)/shard_map/while/body/eval_jaxpr/ppermute | solution.py:20
  579.5 10.4 %collective-permute-start.2 = (f32[5,64,128]{2,1,0:T(8,128)S(1)}, f32[5,64,128]{2,1,0:T(8,128)S(1)}, u32[]{:S(2)}, u32[]{:S(2)}) collective-permute-start(f32[5,64,128]{2,1,0:T(8,128)S(1)} %multiply_add_fusion.11), channel_id=1, source_target_pairs={{120,0},{0,8},{8,16},{16,24},{24,32},{32,40},{40,48},{48,56},{56,6... | collective-permute-start | bytes 491528 | tf_op jit(solution)/shard_map/while/body/eval_jaxpr/ppermute | solution.py:20
  655.9 8.9 %collective-permute-start.3 = (f32[5,64,128]{2,1,0:T(8,128)S(1)}, f32[5,64,128]{2,1,0:T(8,128)S(1)}, u32[]{:S(2)}, u32[]{:S(2)}) collective-permute-start(f32[5,64,128]{2,1,0:T(8,128)S(1)} %multiply_add_fusion.12), channel_id=1, source_target_pairs={{8,0},{16,8},{24,16},{32,24},{40,32},{48,40},{56,48},{64,56},{72,6... | collective-permute-start | bytes 491528 | tf_op jit(solution)/shard_map/while/body/eval_jaxpr/ppermute | solution.py:20
  699.7 8.9 %collective-permute-start.3 = (f32[5,64,128]{2,1,0:T(8,128)S(1)}, f32[5,64,128]{2,1,0:T(8,128)S(1)}, u32[]{:S(2)}, u32[]{:S(2)}) collective-permute-start(f32[5,64,128]{2,1,0:T(8,128)S(1)} %multiply_add_fusion.12), channel_id=1, source_target_pairs={{8,0},{16,8},{24,16},{32,24},{40,32},{48,40},{56,48},{64,56},{72,6... | collective-permute-start | bytes 491528 | tf_op jit(solution)/shard_map/while/body/eval_jaxpr/ppermute | solution.py:20
  708.7 10.0 %collective-permute-start.3 = (f32[5,64,128]{2,1,0:T(8,128)S(1)}, f32[5,64,128]{2,1,0:T(8,128)S(1)}, u32[]{:S(2)}, u32[]{:S(2)}) collective-permute-start(f32[5,64,128]{2,1,0:T(8,128)S(1)} %multiply_add_fusion.12), channel_id=1, source_target_pairs={{8,0},{16,8},{24,16},{32,24},{40,32},{48,40},{56,48},{64,56},{72,6... | collective-permute-start | bytes 491528 | tf_op jit(solution)/shard_map/while/body/eval_jaxpr/ppermute | solution.py:20
  (53 other events, 417.9 us)
where the time goes:
time: 800 us; the launch traced here: 794 us
  waiting for transfers between devices  414 us (52%)
  starting transfers between devices  189 us (24%)
  other arithmetic  98.1 us (12%)
  local copies, waits for them, and re-layouts  54.8 us (7%)
  matrix products  36.4 us (5%)
    ppermute x64, waiting for transfers between devices, from_behind(): return lax.ppermute(block, axis, route)  395 us
    ppermute x64, starting transfers between devices, from_behind(): return lax.ppermute(block, axis, route)  172 us
    add x1, other arithmetic, on_device(): provisional = fluid_state + section_b * new_increment  29.2 us
    dot_general x2, matrix products, solve_lines(): jnp.einsum('ij,vjyz->viyz', lower_table, right_side, precision=highest_pr...  24.1 us
    concatenate x3, other arithmetic, padded_2(): value = jnp.concatenate([before, value, after], axis=dim)  20.6 us
    unnamed x32, local copies, waits for them, and re-layouts  19.3 us
    unnamed x9, other arithmetic  16.6 us
  transfers between devices with their start and end apart: 72, of which 67 were waited for; matrix products, arithmetic and copies ran while one was open for 7% of the time, Pallas kernels for 0%

commit v1 on v0

v1 whole, which is shorter than its diff:
```python
import functools
import math

import jax
import jax.numpy as jnp
from jax import lax
from jax.experimental import pallas as pl
from jax.experimental.pallas import tpu as pltpu
from jax.sharding import PartitionSpec as P

deriv_alpha = 1.0 / 3.0
filter_alpha = 0.4999
gas_gamma = 1.4
time_step = 0.2
section_a = -5.0 / 9.0
section_b = 15.0 / 16.0
MESH = pl.DeviceIdType.MESH
ROWS = 8
FLUX_STEP = 4
NEAR_STEP = 4
UPDATE_STEP = 4
FILTER_STEP = 4
LAST_STEP = 2
VLIM = 56
OUT = pltpu.VMEM
LANES = 128


def root_of(coupling):
    return (-1.0 + math.sqrt(1.0 - 4.0 * coupling * coupling)) / (2.0 * coupling)


deriv_root = root_of(deriv_alpha)
deriv_gain = (
    (25.0 / 36.0)
    / math.sqrt(1.0 - 4.0 * deriv_alpha * deriv_alpha)
    * (1.0 / deriv_root - deriv_root)
)
filter_root = root_of(filter_alpha)


def filter_parts(b):
    w = [
        (93.0 + 70.0 * b) / 128.0,
        (7.0 + 18.0 * b) / 16.0,
        (-7.0 + 14.0 * b) / 32.0,
        (1.0 - 2.0 * b) / 16.0,
        (-1.0 + 2.0 * b) / 128.0,
    ]
    c4 = 8 * w[4]
    c3 = 4 * w[3]
    c2 = 2 * w[2] - 8 * w[4]
    c1 = w[1] - 3 * w[3]
    c0 = w[0] - w[2] + w[4]
    q3 = c4 / (2 * b)
    q2 = (c3 - q3) / (2 * b)
    q1 = (c2 - q2) / (2 * b)
    q0 = (c1 - q1) / (2 * b)
    gain = (c0 - q0) / math.sqrt(1.0 - 4.0 * b * b)
    centre = q0 + q2 / 2 + gain
    return centre, (q1 / 2 + 3 * q3 / 8, q2 / 4, q3 / 8), gain


filter_centre, filter_side, filter_gain = filter_parts(filter_alpha)


def kernel(
    n, zn, rho_h, mom_h, en_h, inc_h,
    Z, S, K2,
    U, FX, FY, FZ, PV, B,
    LP, RP, LR, RR,
    E1, G1, C1, K1, E2, G2, C2,
    in_sem, inc_sem, halo_s, halo_r, self_sem,
    s1, r1, s2, r2, s3, r3, s4, r4,
):
    X = U.shape[1]
    Y = U.shape[2]
    G = Y // ROWS
    V = 5
    per = E1.shape[0] // n
    me = lax.axis_index("gx")
    mey = lax.axis_index("gy")
    mez = lax.axis_index("gz")
    right = lax.rem(me + 1, n)
    left = lax.rem(me + n - 1, n)
    other = 1 - mey
    zup = lax.rem(mez + 1, zn)
    zdown = lax.rem(mez + zn - 1, zn)

    def rows_of(yg):
        return pl.ds(pl.multiple_of(yg * ROWS, ROWS), ROWS)

    def group_at(i):
        return lax.rem(i + G - 1, G)

    def loads(i):
        rows = rows_of(group_at(i))
        return (
            pltpu.make_async_copy(rho_h.at[:, rows, :], U.at[0, :, rows, :], in_sem.at[0, i]),
            pltpu.make_async_copy(mom_h.at[:, :, rows, :], U.at[pl.ds(1, 3), :, rows, :], in_sem.at[1, i]),
            pltpu.make_async_copy(en_h.at[:, rows, :], U.at[4, :, rows, :], in_sem.at[2, i]),
        )

    for i in range(G):
        for c in loads(i):
            c.start()
    inc_load = pltpu.make_async_copy(inc_h, S, inc_sem)
    inc_load.start()

    barrier = pltpu.get_barrier_semaphore()

    def greet(k, _):
        pl.semaphore_signal(
            barrier, inc=1, device_id={"gx": lax.rem(me + k, n)}, device_id_type=MESH
        )
        return 0

    lax.fori_loop(1, n, greet, 0)
    pl.semaphore_signal(barrier, inc=1, device_id={"gy": other}, device_id_type=MESH)
    pl.semaphore_signal(barrier, inc=1, device_id={"gz": zup}, device_id_type=MESH)
    pl.semaphore_signal(barrier, inc=1, device_id={"gz": zdown}, device_id_type=MESH)

    lane = lax.broadcasted_iota(jnp.int32, (ROWS, LANES), 1)
    zero = jnp.zeros((ROWS, LANES), jnp.float32)
    zeros = (zero,) * V

    apart = lax.rem(
        lax.broadcasted_iota(jnp.int32, (2 * LANES, LANES), 0)
        + (2 * LANES - lax.broadcasted_iota(jnp.int32, (2 * LANES, LANES), 1)),
        LANES,
    )
    band = jnp.zeros((2 * LANES, LANES), jnp.float32)
    for o, weight in ((1, 45.0), (2, -9.0), (3, 1.0)):
        band = jnp.where(apart == o, weight, band)
        band = jnp.where(apart == LANES - o, -weight, band)
    B[...] = band.astype(jnp.bfloat16)

    def flux_rows(i, _):
        for c in loads(i):
            c.wait()
        yg = group_at(i)
        rows = rows_of(yg)
        rows_y = pl.ds(pl.multiple_of(yg * ROWS + ROWS, ROWS), ROWS)

        def flux_cells(j, carry):
            ef, g, lp, rp, weight = carry
            ef, g, lp, rp = list(ef), list(g), list(lp), list(rp)
            for u in range(FLUX_STEP):
                x = X - 1 - u - j * FLUX_STEP
                rho = U[0, x, rows, :]
                m0 = U[1, x, rows, :]
                m1 = U[2, x, rows, :]
                m2 = U[3, x, rows, :]
                en = U[4, x, rows, :]
                inv = 1.0 / rho
                v0 = m0 * inv
                v1 = m1 * inv
                v2 = m2 * inv
                a00 = m0 * v0
                a11 = m1 * v1
                a22 = m2 * v2
                a01 = m0 * v1
                a02 = m0 * v2
                a12 = m1 * v2
                pressure = (gas_gamma - 1.0) * (en - 0.5 * (a00 + a11 + a22))
                total = en + pressure
                fx = (m0, a00 + pressure, a01, a02, total * v0)
                fy = (m1, a01, a11 + pressure, a12, total * v1)
                fz = (m2, a02, a12, a22 + pressure, total * v2)
                keep_l = lane < 3 * x + 3
                keep_r = lane < 3 * x + 6
                for v in range(V):
                    FX[v, x + 1, rows, :] = fx[v]
                    FY[v, x, rows_y, :] = fy[v]
                    FZ[v, x, rows, :] = fz[v]
                    Z[v, x, rows, :] = g[v]
                    g[v] = deriv_root * (g[v] + fx[v])
                    ef[v] = ef[v] + weight * fx[v]
                    turned = pltpu.roll(fz[v], 3 * x + 3, 1)
                    lp[v] = jnp.where(keep_l, turned, lp[v])
                    rp[v] = jnp.where(keep_r, turned, rp[v])
                weight = weight * deriv_root
            return tuple(ef), tuple(g), tuple(lp), tuple(rp), weight

        ef, g, lp, rp, _ = lax.fori_loop(
            0, X // FLUX_STEP, flux_cells,
            (zeros, zeros, zeros, zeros, jnp.float32(deriv_root)),
        )
        for v in range(V):
            E1[v * G + yg] = ef[v]
            E1[V * G + v * G + yg] = g[v]
            LP[v, rows, :] = lp[v]
            RP[v, rows, :] = rp[v]
        return 0

    def slot_of(owner, block):
        return jnp.where(owner < n // 2, block, n - 1 - block)

    def chunk(i):
        return pl.ds(i * per, per)

    def ends_copy(E, gathered, ssem, rsem, k):
        owner = lax.rem(me + k, n)
        return pltpu.make_async_remote_copy(
            src_ref=E.at[chunk(owner)],
            dst_ref=gathered.at[chunk(slot_of(owner, me))],
            send_sem=ssem.at[k],
            recv_sem=rsem.at[k],
            device_id={"gx": owner},
            device_id_type=MESH,
        )

    def send_ends(E, gathered, ssem, rsem):
        def one(k, _):
            ends_copy(E, gathered, ssem, rsem, k).start()
            return 0

        lax.fori_loop(1, n, one, 0)
        own = pltpu.make_async_copy(
            E.at[chunk(me)], gathered.at[chunk(slot_of(me, me))], self_sem
        )
        own.start()
        own.wait()

    def carry_copy(C, K, ssem, rsem, k):
        block = lax.rem(me + k, n)
        return pltpu.make_async_remote_copy(
            src_ref=C.at[chunk(slot_of(me, block))],
            dst_ref=K.at[chunk(me)],
            send_sem=ssem.at[k],
            recv_sem=rsem.at[k],
            device_id={"gx": block},
            device_id_type=MESH,
        )

    def wait_all(make):
        def one(k, _):
            make(k).wait()
            return 0

        lax.fori_loop(1, n, one, 0)

    def carries(gathered, C, K, root, ssem, rsem):
        block_root = root**X
        scale = 1.0 / (1.0 - block_root**n)

        def total(s, h):
            return tuple(gathered[s * per + q] + block_root * h[q] for q in range(per))

        h = lax.fori_loop(0, n, total, (zero,) * per)

        def step(s, c):
            for q in range(per):
                C[s * per + q] = c[q]
            return tuple(gathered[s * per + q] + block_root * c[q] for q in range(per))

        lax.fori_loop(0, n, step, tuple(h[q] * scale for q in range(per)))

        def one(k, _):
            carry_copy(C, K, ssem, rsem, k).start()
            return 0

        lax.fori_loop(1, n, one, 0)
        own = pltpu.make_async_copy(
            C.at[chunk(slot_of(me, me))], K.at[chunk(me)], self_sem
        )
        own.start()
        own.wait()

    def remote(src, dst, i, device):
        return pltpu.make_async_remote_copy(
            src_ref=src, dst_ref=dst, send_sem=halo_s.at[i], recv_sem=halo_r.at[i],
            device_id=device, device_id_type=MESH,
        )

    halo = [
        remote(LP, LR, 0, {"gz": zup}),
        remote(RP, RR, 1, {"gz": zdown}),
        remote(FY.at[:, :, pl.ds(Y, ROWS), :], FY.at[:, :, pl.ds(0, ROWS), :], 2, {"gy": other}),
        remote(FY.at[:, :, pl.ds(ROWS, ROWS), :], FY.at[:, :, pl.ds(Y + ROWS, ROWS), :], 3, {"gy": other}),
        remote(FX.at[:, pl.ds(X, 1)], FX.at[:, pl.ds(0, 1)], 4, {"gx": right}),
        remote(FX.at[:, pl.ds(1, 1)], FX.at[:, pl.ds(X + 1, 1)], 5, {"gx": left}),
    ]
    lax.fori_loop(0, 2, flux_rows, 0)
    pl.semaphore_wait(barrier, n + 2)
    halo[2].start()
    halo[3].start()
    lax.fori_loop(2, G, flux_rows, 0)
    send_ends(E1, G1, s1, r1)
    for i in (0, 1, 4, 5):
        halo[i].start()

    inc_load.wait()
    halo[2].wait()
    halo[3].wait()
    k1, k2, k3 = (-time_step * w for w in (0.75, -0.15, 1.0 / 60.0))

    z_scale = -time_step / 60.0

    def yz_plane(x, _):
        hz = FZ[:, x].reshape(V * Y, LANES)
        head = hz.astype(jnp.bfloat16)
        rest = hz - head.astype(jnp.float32)
        middle = rest.astype(jnp.bfloat16)
        tail = (rest - middle.astype(jnp.float32)).astype(jnp.bfloat16)
        dz = jnp.dot(
            jnp.concatenate([head, middle], axis=1), B[...], preferred_element_type=jnp.float32
        ) + jnp.dot(tail, B[0:LANES, :], preferred_element_type=jnp.float32)
        for v in range(V):
            for yg in range(G):
                base = ROWS + yg * ROWS
                out = slice(yg * ROWS, yg * ROWS + ROWS)
                at = v * Y + yg * ROWS

                def both(o):
                    return (
                        FY[v, x, base + o : base + o + ROWS, :]
                        - FY[v, x, base - o : base - o + ROWS, :]
                    )

                S[v, x, out, :] = (
                    (section_a * S[v, x, out, :] + z_scale * dz[at : at + ROWS, :])
                    + (k1 * both(1) + k2 * both(2) + k3 * both(3))
                )
        return 0

    lax.fori_loop(0, X, yz_plane, 0)

    wait_all(lambda k: ends_copy(E1, G1, s1, r1, k))
    carries(G1, C1, K1, deriv_root, s2, r2)

    halo[0].wait()
    halo[1].wait()
    third = lax.rem(lane, 3)
    weights = (k1, k2, k3)

    def z_edges(v, _):
        for yg in range(G):
            rows = slice(yg * ROWS, yg * ROWS + ROWS)
            dl = LR[v, rows, :] - LP[v, rows, :]
            dr = RR[v, rows, :] - RP[v, rows, :]
            low = zero
            high = zero
            for o in (1, 2, 3):
                low = low - jnp.where(third < o, weights[o - 1] * pltpu.roll(dl, o, 1), 0.0)
                high = high + jnp.where(
                    third >= 3 - o, weights[o - 1] * pltpu.roll(dr, LANES - o, 1), 0.0
                )
            LR[v, rows, :] = low
            RR[v, rows, :] = high
        return 0

    lax.fori_loop(0, V, z_edges, 0)

    halo[4].wait()
    halo[5].wait()
    near = -time_step / 12.0
    far = -time_step * deriv_gain

    def near_rows(yg, _):
        rows = rows_of(yg)
        low = [LR[v, rows, :] for v in range(V)]
        high = [RR[v, rows, :] for v in range(V)]
        rim = (lane < 3) | (lane >= LANES - 3)

        def near_cells(j, f):
            f = list(f)
            x0 = j * NEAR_STEP
            for v in range(V):
                window = [FX[v, x0 + u, rows, :] for u in range(NEAR_STEP + 2)]
                for u in range(NEAR_STEP):
                    x = x0 + u
                    edge = jnp.where(lane < 3 * x + 3, high[v], low[v])
                    edge = jnp.where(rim, pltpu.roll(edge, 125 - 3 * x, 1), 0.0)
                    S[v, x, rows, :] = (
                        (S[v, x, rows, :] + edge)
                        + near * (window[u + 2] - window[u])
                        + far * (Z[v, x, rows, :] - f[v])
                    )
                    f[v] = deriv_root * (f[v] + window[u + 1])
            return tuple(f)

        lax.fori_loop(0, X // NEAR_STEP, near_cells, zeros)
        return 0

    lax.fori_loop(0, G, near_rows, 0)

    wait_all(lambda k: carry_copy(C1, K1, s2, r2, k))

    def update_rows(yg, _):
        rows = rows_of(yg)
        cf = [(-far * deriv_root ** (X - 1)) * K1[v * G + yg] for v in range(V)]
        cb = [far * K1[V * G + v * G + yg] for v in range(V)]

        def update_cells(j, carry):
            ef, g, wf, wb, weight = carry
            ef, g = list(ef), list(g)
            for u in range(UPDATE_STEP):
                x = X - 1 - u - j * UPDATE_STEP
                for v in range(V):
                    s = S[v, x, rows, :] + (wf * cf[v] + wb * cb[v])
                    p = U[v, x, rows, :] + section_b * s
                    S[v, x, rows, :] = s
                    PV[v, x + 3, rows, :] = p
                    Z[v, x, rows, :] = g[v]
                    g[v] = filter_root * (g[v] + p)
                    ef[v] = ef[v] + weight * p
                wf = wf * (1.0 / deriv_root)
                wb = wb * deriv_root
                weight = weight * filter_root
            return tuple(ef), tuple(g), wf, wb, weight

        ef, g, _, _, _ = lax.fori_loop(
            0, X // UPDATE_STEP, update_cells,
            (zeros, zeros, jnp.float32(1.0), jnp.float32(1.0), jnp.float32(filter_root)),
        )
        for v in range(V):
            E2[v * G + yg] = ef[v]
            E2[V * G + v * G + yg] = g[v]
        return 0

    lax.fori_loop(0, G, update_rows, 0)

    send_ends(E2, G2, s3, r3)
    sides = [
        remote(PV.at[:, pl.ds(X, 3)], PV.at[:, pl.ds(0, 3)], 6, {"gx": right}),
        remote(PV.at[:, pl.ds(3, 3)], PV.at[:, pl.ds(X + 3, 3)], 7, {"gx": left}),
    ]
    for c in sides:
        c.start()

    wait_all(lambda k: ends_copy(E2, G2, s3, r3, k))
    carries(G2, C2, K2, filter_root, s4, r4)

    sides[0].wait()
    sides[1].wait()
    t1, t2, t3 = filter_side

    def filter_rows(yg, _):
        rows = rows_of(yg)

        def filter_cells(j, f):
            f = list(f)
            x0 = j * FILTER_STEP
            for v in range(V):
                w = [PV[v, x0 + u, rows, :] for u in range(FILTER_STEP + 6)]
                for u in range(FILTER_STEP):
                    x = x0 + u
                    Z[v, x, rows, :] = (
                        filter_centre * w[u + 3]
                        + filter_gain * (Z[v, x, rows, :] + f[v])
                        + t1 * (w[u + 4] + w[u + 2])
                        + t2 * (w[u + 5] + w[u + 1])
                        + t3 * (w[u + 6] + w[u])
                    )
                    f[v] = filter_root * (f[v] + w[u + 3])
            return tuple(f)

        lax.fori_loop(0, X // FILTER_STEP, filter_cells, zeros)
        return 0

    lax.fori_loop(0, G, filter_rows, 0)
    wait_all(lambda k: carry_copy(C2, K2, s4, r4, k))


def last_kernel(z_ref, s_ref, carry_ref, state_h, inc_h, out, sem):
    X = z_ref.shape[1]
    G = z_ref.shape[2] // ROWS
    inc_out = pltpu.make_async_copy(s_ref, inc_h, sem.at[X // LAST_STEP])
    parts = X // LAST_STEP

    def state_out(j):
        planes = pl.ds(j * LAST_STEP, LAST_STEP)
        return pltpu.make_async_copy(out.at[:, planes], state_h.at[:, planes], sem.at[j])

    inc_out.start()
    for j in range(parts):
        for v in range(5):
            for yg in range(G):
                rows = slice(yg * ROWS, yg * ROWS + ROWS)
                ahead = carry_ref[v * G + yg]
                behind = carry_ref[(5 + v) * G + yg]
                for u in range(LAST_STEP):
                    x = j * LAST_STEP + u
                    out[v, x, rows, :] = z_ref[v, x, rows, :] + (
                        (filter_gain * filter_root**x) * ahead
                        + (filter_gain * filter_root ** (X - 1 - x)) * behind
                    )
        state_out(j).start()
    for j in range(parts):
        state_out(j).wait()
    inc_out.wait()


def section(n, zn, density, momentum, energy, increment):
    X, Y, L = density.shape
    G = Y // ROWS
    ends = 2 * 5 * G
    f32 = jnp.float32
    pack = pltpu.VMEM((5, Y, L), f32)
    end = pltpu.VMEM((ends, ROWS, L), f32)
    many = pltpu.SemaphoreType.DMA((n,))
    anywhere = pl.BlockSpec(memory_space=pl.ANY)
    hbm = pl.BlockSpec(memory_space=pltpu.HBM)
    vmem = pl.BlockSpec(memory_space=pltpu.VMEM)
    part, register, carry = pl.pallas_call(
        functools.partial(kernel, n, zn),
        out_shape=(
            OUT((5, X, Y, L), f32),
            OUT((5, X, Y, L), f32),
            OUT((ends, ROWS, L), f32),
        ),
        in_specs=[hbm] * 4,
        out_specs=(vmem,) * 3,
        scratch_shapes=[
            pltpu.VMEM((5, X, Y, L), f32),
            pltpu.VMEM((5, X + 2, Y, L), f32),
            pltpu.VMEM((5, X, Y + 2 * ROWS, L), f32),
            pltpu.VMEM((5, X, Y, L), f32),
            pltpu.VMEM((5, X + 6, Y, L), f32),
            pltpu.VMEM((2 * L, L), jnp.bfloat16),
            pack, pack, pack, pack,
            end, end, end, end, end, end, end,
            pltpu.SemaphoreType.DMA((3, G)),
            pltpu.SemaphoreType.DMA,
            pltpu.SemaphoreType.DMA((8,)),
            pltpu.SemaphoreType.DMA((8,)),
            pltpu.SemaphoreType.DMA,
            many, many, many, many, many, many, many, many,
        ],
        compiler_params=pltpu.CompilerParams(
            collective_id=0, has_side_effects=True, vmem_limit_bytes=VLIM * 1024 * 1024
        ),
    )(density, momentum, energy, increment)
    return pl.pallas_call(
        last_kernel,
        out_shape=(
            jax.ShapeDtypeStruct((5, X, Y, L), f32),
            jax.ShapeDtypeStruct((5, X, Y, L), f32),
        ),
        in_specs=[vmem] * 3,
        out_specs=(hbm, hbm),
        scratch_shapes=[
            pltpu.VMEM((5, X, Y, L), f32),
            pltpu.SemaphoreType.DMA((X // LAST_STEP + 1,)),
        ],
        compiler_params=pltpu.CompilerParams(vmem_limit_bytes=16 * 1024 * 1024),
    )(part, register, carry)


def solution(mesh):
    in_specs = (
        P("gx", "gy", "gz"),
        P(None, "gx", "gy", "gz"),
        P("gx", "gy", "gz"),
        P(None, "gx", "gy", "gz"),
    )
    out_specs = (P(None, "gx", "gy", "gz"), P(None, "gx", "gy", "gz"))
    return jax.shard_map(
        functools.partial(section, mesh.shape["gx"], mesh.shape["gz"]),
        mesh=mesh,
        in_specs=in_specs,
        out_specs=out_specs,
        check_vma=False,
    )
```

time: 800 us -> 55.6 us (0.07)
  waiting for transfers between devices: 414 us -> 0 us
  starting transfers between devices: 189 us -> 0 us
  other arithmetic: 98.1 us -> 0 us
  Pallas kernels: 0 us -> 54.9 us
  local copies, waits for them, and re-layouts: 54.8 us -> 0 us
  matrix products: 36.4 us -> 0 us
    ppermute x72 -> x0, waiting for transfers between devices: 414 us -> none  [the longest x64 395 us: from_behind(): return lax.ppermute(block, axis, route)]
    ppermute x72 -> x0, starting transfers between devices: 189 us -> none  [the longest x64 172 us: from_behind(): return lax.ppermute(block, axis, route)]
    pallas_call x0 -> x2, Pallas kernels: none -> 54.9 us  [the longest x1 51.6 us: section(): pl.pallas_call(functools.partial(kernel, n, zn), out_shape=(OUT((5, X, Y,...]
    add x65 -> x0, other arithmetic: 51.9 us -> none  [the longest x1 29.2 us: on_device(): provisional = fluid_state + section_b * new_increment]
    dot_general x4 -> x0, matrix products: 36.4 us -> none  [the longest x2 24.1 us: solve_lines(): jnp.einsum('ij,vjyz->viyz', lower_table, right_side, precision=highest_pr...]
    slice x11 -> x0, local copies, waits for them, and re-layouts: 21.5 us -> none  [the longest x4 12.2 us: padded_2(): last = lax.slice_in_dim(value, length - width, length, axis=dim)]
    concatenate x4 -> x0, other arithmetic: 20.9 us -> none  [the longest x3 20.6 us: padded_2(): value = jnp.concatenate([before, value, after], axis=dim)]
    unnamed x32 -> x0, local copies, waits for them, and re-layouts: 19.3 us -> none
  transfers between devices with their start and end apart: 72 -> 0, of which waited for: 67 -> 0; matrix products, arithmetic and copies ran while one was open for 7% -> 0% of each run, Pallas kernels for 0% -> 0%
where the time goes in v1:
time: 55.6 us; the launch traced here: 55.5 us
  Pallas kernels  54.9 us (99%)
  between operations  0.64 us (1%)
    pallas_call x1, Pallas kernels, section(): pl.pallas_call(functools.partial(kernel, n, zn), out_shape=(OUT((5, X, Y,...  51.6 us
    pallas_call x1, Pallas kernels, section(): pl.pallas_call(last_kernel, out_shape=(jax.ShapeDtypeStruct((5, X, Y, L),...  3.23 us

profile of v1, /device:TPU:0, one launch (start us, length us, event | category | flops | bytes accessed | tf_op | source)
XLA Modules:
  0.0 55.5 jit_solution(3744421543693898376)
XLA Ops:
  0.6 51.6 %shard_map.59 = (f32[5,24,64,128]{3,2,1,0:T(8,128)S(1)}, f32[5,24,64,128]{3,2,1,0:T(8,128)S(1)}, f32[80,8,128]{2,1,0:T(8,128)S(1)}) custom-call(f32[24,64,128]{2,1,0:T(8,128)} %rho_h.1, f32[3,24,64,128]{3,2,1,0:T(8,128)} %mom_h.1, f32[24,64,128]{2,1,0:T(8,128)} %en_h.1, f32[5,24,64,128]{3,2,1,0:T(8,128)} %inc_h.1), custom_call_target="tpu_custom_call" | custom-call | tf_op jit(solution)/shard_map/pallas_call | solution.py:506
  52.3 3.2 %shard_map.60 = (f32[5,24,64,128]{3,2,1,0:T(8,128)}, f32[5,24,64,128]{3,2,1,0:T(8,128)}) custom-call(f32[5,24,64,128]{3,2,1,0:T(8,128)S(1)} %get-tuple-element.5.z_ref, f32[5,24,64,128]{3,2,1,0:T(8,128)S(1)} %get-tuple-element.6.s_ref, f32[80,8,128]{2,1,0:T(8,128)S(1)} %get-tuple-element.7.carry_ref), custom_call_target="tpu_custom_call" | custom-call | tf_op jit(solution)/shard_map/pallas_call | solution.py:535

commit v2 on v1

--- a/solution.py
+++ b/solution.py
@@ -17,9 +17,9 @@
 MESH = pl.DeviceIdType.MESH
 ROWS = 8
 FLUX_STEP = 4
-NEAR_STEP = 4
+NEAR_STEP = 3
 UPDATE_STEP = 4
-FILTER_STEP = 4
+FILTER_STEP = 3
 LAST_STEP = 2
 VLIM = 56
 OUT = pltpu.VMEM
@@ -70,14 +70,17 @@
     U, FX, FY, FZ, PV, B,
     LP, RP, LR, RR,
     E1, G1, C1, K1, E2, G2, C2,
-    in_sem, inc_sem, halo_s, halo_r, self_sem,
+    PE, FT, CN, DN,
+    in_sem, inc_sem, halo_s, halo_r,
     s1, r1, s2, r2, s3, r3, s4, r4,
 ):
     X = U.shape[1]
     Y = U.shape[2]
     G = Y // ROWS
     V = 5
+    T = X - 3
     per = E1.shape[0] // n
+    order = sorted(range(1, n), key=lambda k: (-min(k % 4, 4 - k % 4) - min(k // 4, 4 - k // 4), k))
     me = lax.axis_index("gx")
     mey = lax.axis_index("gy")
     mez = lax.axis_index("gz")
@@ -167,6 +170,7 @@
                 fx = (m0, a00 + pressure, a01, a02, total * v0)
                 fy = (m1, a01, a11 + pressure, a12, total * v1)
                 fz = (m2, a02, a12, a22 + pressure, total * v2)
+                now = jnp.where(x < T, weight, 0.0)
                 keep_l = lane < 3 * x + 3
                 keep_r = lane < 3 * x + 6
                 for v in range(V):
@@ -175,11 +179,11 @@
                     FZ[v, x, rows, :] = fz[v]
                     Z[v, x, rows, :] = g[v]
                     g[v] = deriv_root * (g[v] + fx[v])
-                    ef[v] = ef[v] + weight * fx[v]
+                    ef[v] = ef[v] + now * fx[v]
                     turned = pltpu.roll(fz[v], 3 * x + 3, 1)
                     lp[v] = jnp.where(keep_l, turned, lp[v])
                     rp[v] = jnp.where(keep_r, turned, rp[v])
-                weight = weight * deriv_root
+                weight = jnp.where(x < T, weight * deriv_root, weight)
             return tuple(ef), tuple(g), tuple(lp), tuple(rp), weight
 
         ef, g, lp, rp, _ = lax.fori_loop(
@@ -187,7 +191,11 @@
             (zeros, zeros, zeros, zeros, jnp.float32(deriv_root)),
         )
         for v in range(V):
-            E1[v * G + yg] = ef[v]
+            FT[v * G + yg] = ef[v]
+            f = ef[v]
+            for x in range(T, X):
+                f = deriv_root * (f + FX[v, x + 1, rows, :])
+            E1[v * G + yg] = f
             E1[V * G + v * G + yg] = g[v]
             LP[v, rows, :] = lp[v]
             RP[v, rows, :] = rp[v]
@@ -210,17 +218,14 @@
             device_id_type=MESH,
         )
 
+    def keep_own(src, dst, start, end):
+        for q in range(per):
+            dst[end * per + q] = src[start * per + q]
+
     def send_ends(E, gathered, ssem, rsem):
-        def one(k, _):
+        for k in order:
             ends_copy(E, gathered, ssem, rsem, k).start()
-            return 0
-
-        lax.fori_loop(1, n, one, 0)
-        own = pltpu.make_async_copy(
-            E.at[chunk(me)], gathered.at[chunk(slot_of(me, me))], self_sem
-        )
-        own.start()
-        own.wait()
+        keep_own(E, gathered, me, slot_of(me, me))
 
     def carry_copy(C, K, ssem, rsem, k):
         block = lax.rem(me + k, n)
@@ -256,16 +261,9 @@
 
         lax.fori_loop(0, n, step, tuple(h[q] * scale for q in range(per)))
 
-        def one(k, _):
+        for k in order:
             carry_copy(C, K, ssem, rsem, k).start()
-            return 0
-
-        lax.fori_loop(1, n, one, 0)
-        own = pltpu.make_async_copy(
-            C.at[chunk(slot_of(me, me))], K.at[chunk(me)], self_sem
-        )
-        own.start()
-        own.wait()
+        keep_own(C, K, slot_of(me, me), me)
 
     def remote(src, dst, i, device):
         return pltpu.make_async_remote_copy(
@@ -281,12 +279,11 @@
         remote(FX.at[:, pl.ds(X, 1)], FX.at[:, pl.ds(0, 1)], 4, {"gx": right}),
         remote(FX.at[:, pl.ds(1, 1)], FX.at[:, pl.ds(X + 1, 1)], 5, {"gx": left}),
     ]
-    lax.fori_loop(0, 2, flux_rows, 0)
+    lax.fori_loop(0, G, flux_rows, 0)
     pl.semaphore_wait(barrier, n + 2)
+    send_ends(E1, G1, s1, r1)
     halo[2].start()
     halo[3].start()
-    lax.fori_loop(2, G, flux_rows, 0)
-    send_ends(E1, G1, s1, r1)
     for i in (0, 1, 4, 5):
         halo[i].start()
 
@@ -324,10 +321,11 @@
                 )
         return 0
 
-    lax.fori_loop(0, X, yz_plane, 0)
+    lax.fori_loop(0, 16, yz_plane, 0)
 
     wait_all(lambda k: ends_copy(E1, G1, s1, r1, k))
     carries(G1, C1, K1, deriv_root, s2, r2)
+    lax.fori_loop(16, X, yz_plane, 0)
 
     halo[0].wait()
     halo[1].wait()
@@ -356,36 +354,72 @@
     halo[5].wait()
     near = -time_step / 12.0
     far = -time_step * deriv_gain
+    rim = (lane < 3) | (lane >= LANES - 3)
+
+    def near_cells(rows, v, x0, count, f, low, high):
+        window = [FX[v, x0 + u, rows, :] for u in range(count + 2)]
+        out = []
+        for u in range(count):
+            x = x0 + u
+            edge = jnp.where(lane < 3 * x + 3, high, low)
+            edge = jnp.where(rim, pltpu.roll(edge, 125 - 3 * x, 1), 0.0)
+            s = (
+                (S[v, x, rows, :] + edge)
+                + near * (window[u + 2] - window[u])
+                + far * (Z[v, x, rows, :] - f)
+            )
+            S[v, x, rows, :] = s
+            out.append(s)
+            f = deriv_root * (f + window[u + 1])
+        return f, out
+
+    def outer_rows(yg, _):
+        rows = rows_of(yg)
+        for v in range(V):
+            low = LR[v, rows, :]
+            high = RR[v, rows, :]
+            for side, x0, f in ((0, T, FT[v * G + yg]), (1, 0, zero)):
+                _, found = near_cells(rows, v, x0, 3, f, low, high)
+                for u in range(3):
+                    PE[side, v, u, rows, :] = U[v, x0 + u, rows, :] + section_b * found[u]
+        return 0
+
+    lax.fori_loop(0, G, outer_rows, 0)
+    sides = [
+        remote(PE.at[0], PV.at[:, pl.ds(0, 3)], 6, {"gx": right}),
+        remote(PE.at[1], PV.at[:, pl.ds(X + 3, 3)], 7, {"gx": left}),
+    ]
+    sides[0].start()
+    sides[1].start()
 
     def near_rows(yg, _):
         rows = rows_of(yg)
         low = [LR[v, rows, :] for v in range(V)]
         high = [RR[v, rows, :] for v in range(V)]
-        rim = (lane < 3) | (lane >= LANES - 3)
-
-        def near_cells(j, f):
-            f = list(f)
-            x0 = j * NEAR_STEP
-            for v in range(V):
-                window = [FX[v, x0 + u, rows, :] for u in range(NEAR_STEP + 2)]
-                for u in range(NEAR_STEP):
-                    x = x0 + u
-                    edge = jnp.where(lane < 3 * x + 3, high[v], low[v])
-                    edge = jnp.where(rim, pltpu.roll(edge, 125 - 3 * x, 1), 0.0)
-                    S[v, x, rows, :] = (
-                        (S[v, x, rows, :] + edge)
-                        + near * (window[u + 2] - window[u])
-                        + far * (Z[v, x, rows, :] - f[v])
-                    )
-                    f[v] = deriv_root * (f[v] + window[u + 1])
-            return tuple(f)
-
-        lax.fori_loop(0, X // NEAR_STEP, near_cells, zeros)
+        start = []
+        for v in range(V):
+            f = zero
+            for x in range(3):
+                f = deriv_root * (f + FX[v, x + 1, rows, :])
+            start.append(f)
+
+        def cells(j, f):
+            x0 = 3 + j * NEAR_STEP
+            return tuple(
+                near_cells(rows, v, x0, NEAR_STEP, f[v], low[v], high[v])[0] for v in range(V)
+            )
+
+        lax.fori_loop(0, (X - 6) // NEAR_STEP, cells, tuple(start))
         return 0
 
     lax.fori_loop(0, G, near_rows, 0)
 
     wait_all(lambda k: carry_copy(C1, K1, s2, r2, k))
+    lines = V * G
+    beyond = [
+        remote(K1.at[pl.ds(0, lines)], CN, 8, {"gx": right}),
+        remote(K1.at[pl.ds(lines, lines)], DN, 9, {"gx": left}),
+    ]
 
     def update_rows(yg, _):
         rows = rows_of(yg)
@@ -422,26 +456,23 @@
     lax.fori_loop(0, G, update_rows, 0)
 
     send_ends(E2, G2, s3, r3)
-    sides = [
-        remote(PV.at[:, pl.ds(X, 3)], PV.at[:, pl.ds(0, 3)], 6, {"gx": right}),
-        remote(PV.at[:, pl.ds(3, 3)], PV.at[:, pl.ds(X + 3, 3)], 7, {"gx": left}),
-    ]
-    for c in sides:
-        c.start()
-
-    wait_all(lambda k: ends_copy(E2, G2, s3, r3, k))
-    carries(G2, C2, K2, filter_root, s4, r4)
-
-    sides[0].wait()
-    sides[1].wait()
+    beyond[0].start()
+    beyond[1].start()
     t1, t2, t3 = filter_side
 
     def filter_rows(yg, _):
         rows = rows_of(yg)
+        start = []
+        for v in range(V):
+            f = zero
+            for x in range(3):
+                Z[v, x, rows, :] = filter_gain * (Z[v, x, rows, :] + f)
+                f = filter_root * (f + PV[v, x + 3, rows, :])
+            start.append(f)
 
         def filter_cells(j, f):
             f = list(f)
-            x0 = j * FILTER_STEP
+            x0 = 3 + j * FILTER_STEP
             for v in range(V):
                 w = [PV[v, x0 + u, rows, :] for u in range(FILTER_STEP + 6)]
                 for u in range(FILTER_STEP):
@@ -456,10 +487,58 @@
                     f[v] = filter_root * (f[v] + w[u + 3])
             return tuple(f)
 
-        lax.fori_loop(0, X // FILTER_STEP, filter_cells, zeros)
+        f = lax.fori_loop(0, (X - 6) // FILTER_STEP, filter_cells, tuple(start))
+        for v in range(V):
+            last = f[v]
+            for x in range(T, X):
+                Z[v, x, rows, :] = filter_gain * (Z[v, x, rows, :] + last)
+                last = filter_root * (last + PV[v, x + 3, rows, :])
         return 0
 
     lax.fori_loop(0, G, filter_rows, 0)
+
+    wait_all(lambda k: ends_copy(E2, G2, s3, r3, k))
+    carries(G2, C2, K2, filter_root, s4, r4)
+
+    for c in (*sides, *beyond):
+        c.wait()
+    block_root = deriv_root**X
+    ahead_gain = [-section_b * far * deriv_root**x for x in range(X)]
+    behind_gain = [section_b * far * deriv_root ** (X - 1 - x) for x in range(X)]
+
+    def end_rows(yg, _):
+        rows = rows_of(yg)
+        for v in range(V):
+            q = v * G + yg
+            left_c = CN[q]
+            left_d = E1[lines + q] + block_root * K1[lines + q]
+            right_c = E1[q] + block_root * K1[q]
+            right_d = DN[q]
+            w = []
+            for u in range(3):
+                w.append(
+                    PV[v, u, rows, :]
+                    + (ahead_gain[T + u] * left_c + behind_gain[T + u] * left_d)
+                )
+            w += [PV[v, 3 + u, rows, :] for u in range(6)]
+            w2 = [PV[v, X - 3 + u, rows, :] for u in range(6)]
+            for u in range(3):
+                w2.append(
+                    PV[v, X + 3 + u, rows, :]
+                    + (ahead_gain[u] * right_c + behind_gain[u] * right_d)
+                )
+            for x0, w in ((0, w), (T, w2)):
+                for u in range(3):
+                    Z[v, x0 + u, rows, :] = (
+                        Z[v, x0 + u, rows, :]
+                        + filter_centre * w[u + 3]
+                        + t1 * (w[u + 4] + w[u + 2])
+                        + t2 * (w[u + 5] + w[u + 1])
+                        + t3 * (w[u + 6] + w[u])
+                    )
+        return 0
+
+    lax.fori_loop(0, G, end_rows, 0)
     wait_all(lambda k: carry_copy(C2, K2, s4, r4, k))
 
 
@@ -499,6 +578,7 @@
     f32 = jnp.float32
     pack = pltpu.VMEM((5, Y, L), f32)
     end = pltpu.VMEM((ends, ROWS, L), f32)
+    half = pltpu.VMEM((ends // 2, ROWS, L), f32)
     many = pltpu.SemaphoreType.DMA((n,))
     anywhere = pl.BlockSpec(memory_space=pl.ANY)
     hbm = pl.BlockSpec(memory_space=pltpu.HBM)
@@ -521,11 +601,12 @@
             pltpu.VMEM((2 * L, L), jnp.bfloat16),
             pack, pack, pack, pack,
             end, end, end, end, end, end, end,
+            pltpu.VMEM((2, 5, 3, Y, L), f32),
+            half, half, half,
             pltpu.SemaphoreType.DMA((3, G)),
             pltpu.SemaphoreType.DMA,
-            pltpu.SemaphoreType.DMA((8,)),
-            pltpu.SemaphoreType.DMA((8,)),
-            pltpu.SemaphoreType.DMA,
+            pltpu.SemaphoreType.DMA((10,)),
+            pltpu.SemaphoreType.DMA((10,)),
             many, many, many, many, many, many, many, many,
         ],
         compiler_params=pltpu.CompilerParams(

time: 55.6 us -> 51.4 us (0.924)
  Pallas kernels: 54.9 us -> 50.2 us
    pallas_call x1, Pallas kernels: 51.6 us -> 47 us  [section(): pl.pallas_call(functools.partial(kernel, n, zn), out_shape=(OUT((5, X, Y,...]
where the time goes in v2:
time: 51.4 us; the launch traced here: 50.9 us
  Pallas kernels  50.2 us (98%)
  between operations  0.64 us (1%)
    pallas_call x1, Pallas kernels, section(): pl.pallas_call(functools.partial(kernel, n, zn), out_shape=(OUT((5, X, Y,...  47 us
    pallas_call x1, Pallas kernels, section(): pl.pallas_call(last_kernel, out_shape=(jax.ShapeDtypeStruct((5, X, Y, L),...  3.23 us

profile of v2, /device:TPU:0, one launch (start us, length us, event | category | flops | bytes accessed | tf_op | source)
XLA Modules:
  0.0 50.9 jit_solution(6982817900257571650)
XLA Ops:
  0.6 47.0 %shard_map.59 = (f32[5,24,64,128]{3,2,1,0:T(8,128)S(1)}, f32[5,24,64,128]{3,2,1,0:T(8,128)S(1)}, f32[80,8,128]{2,1,0:T(8,128)S(1)}) custom-call(f32[24,64,128]{2,1,0:T(8,128)} %rho_h.1, f32[3,24,64,128]{3,2,1,0:T(8,128)} %mom_h.1, f32[24,64,128]{2,1,0:T(8,128)} %en_h.1, f32[5,24,64,128]{3,2,1,0:T(8,128)} %inc_h.1), custom_call_target="tpu_custom_call" | custom-call | tf_op jit(solution)/shard_map/pallas_call | solution.py:586
  47.7 3.2 %shard_map.60 = (f32[5,24,64,128]{3,2,1,0:T(8,128)}, f32[5,24,64,128]{3,2,1,0:T(8,128)}) custom-call(f32[5,24,64,128]{3,2,1,0:T(8,128)S(1)} %get-tuple-element.5.z_ref, f32[5,24,64,128]{3,2,1,0:T(8,128)S(1)} %get-tuple-element.6.s_ref, f32[80,8,128]{2,1,0:T(8,128)S(1)} %get-tuple-element.7.carry_ref), custom_call_target="tpu_custom_call" | custom-call | tf_op jit(solution)/shard_map/pallas_call | solution.py:616

commit v3 on v2

--- a/solution.py
+++ b/solution.py
@@ -16,12 +16,13 @@
 section_b = 15.0 / 16.0
 MESH = pl.DeviceIdType.MESH
 ROWS = 8
-FLUX_STEP = 4
-NEAR_STEP = 3
-UPDATE_STEP = 4
-FILTER_STEP = 3
+FLUX_STEP = 6
+NEAR_STEP = 6
+UPDATE_STEP = 6
+FILTER_STEP = 6
 LAST_STEP = 2
 VLIM = 56
+YZ_SPLIT = 16
 OUT = pltpu.VMEM
 LANES = 128
 
@@ -294,7 +295,8 @@
 
     z_scale = -time_step / 60.0
 
-    def yz_plane(x, _):
+    def yz_plane(i, _):
+        x = jnp.where(i < 3, i, jnp.where(i < 6, i + X - 6, i - 3))
         hz = FZ[:, x].reshape(V * Y, LANES)
         head = hz.astype(jnp.bfloat16)
         rest = hz - head.astype(jnp.float32)
@@ -321,11 +323,10 @@
                 )
         return 0
 
-    lax.fori_loop(0, 16, yz_plane, 0)
+    lax.fori_loop(0, YZ_SPLIT, yz_plane, 0)
 
     wait_all(lambda k: ends_copy(E1, G1, s1, r1, k))
     carries(G1, C1, K1, deriv_root, s2, r2)
-    lax.fori_loop(16, X, yz_plane, 0)
 
     halo[0].wait()
     halo[1].wait()
@@ -391,6 +392,7 @@
     ]
     sides[0].start()
     sides[1].start()
+    lax.fori_loop(YZ_SPLIT, X, yz_plane, 0)
 
     def near_rows(yg, _):
         rows = rows_of(yg)

time: 51.4 us -> 50.3 us (0.979)
  Pallas kernels: 50.2 us -> 49.2 us
    pallas_call x1, Pallas kernels: 47 us -> 46 us  [section(): pl.pallas_call(functools.partial(kernel, n, zn), out_shape=(OUT((5, X, Y,...]
where the time goes in v3:
time: 50.3 us; the launch traced here: 49.9 us
  Pallas kernels  49.2 us (98%)
  between operations  0.64 us (1%)
    pallas_call x1, Pallas kernels, section(): pl.pallas_call(functools.partial(kernel, n, zn), out_shape=(OUT((5, X, Y,...  46 us
    pallas_call x1, Pallas kernels, section(): pl.pallas_call(last_kernel, out_shape=(jax.ShapeDtypeStruct((5, X, Y, L),...  3.23 us

profile of v3, /device:TPU:0, one launch (start us, length us, event | category | flops | bytes accessed | tf_op | source)
XLA Modules:
  0.0 49.9 jit_solution(15630913551331605381)
XLA Ops:
  0.6 46.0 %shard_map.59 = (f32[5,24,64,128]{3,2,1,0:T(8,128)S(1)}, f32[5,24,64,128]{3,2,1,0:T(8,128)S(1)}, f32[80,8,128]{2,1,0:T(8,128)S(1)}) custom-call(f32[24,64,128]{2,1,0:T(8,128)} %rho_h.1, f32[3,24,64,128]{3,2,1,0:T(8,128)} %mom_h.1, f32[24,64,128]{2,1,0:T(8,128)} %en_h.1, f32[5,24,64,128]{3,2,1,0:T(8,128)} %inc_h.1), custom_call_target="tpu_custom_call" | custom-call | tf_op jit(solution)/shard_map/pallas_call | solution.py:588
  46.6 3.2 %shard_map.60 = (f32[5,24,64,128]{3,2,1,0:T(8,128)}, f32[5,24,64,128]{3,2,1,0:T(8,128)}) custom-call(f32[5,24,64,128]{3,2,1,0:T(8,128)S(1)} %get-tuple-element.5.z_ref, f32[5,24,64,128]{3,2,1,0:T(8,128)S(1)} %get-tuple-element.6.s_ref, f32[80,8,128]{2,1,0:T(8,128)S(1)} %get-tuple-element.7.carry_ref), custom_call_target="tpu_custom_call" | custom-call | tf_op jit(solution)/shard_map/pallas_call | solution.py:618

commit v4 on v3

--- a/solution.py
+++ b/solution.py
@@ -16,9 +16,9 @@
 section_b = 15.0 / 16.0
 MESH = pl.DeviceIdType.MESH
 ROWS = 8
-FLUX_STEP = 6
+FLUX_STEP = 8
 NEAR_STEP = 6
-UPDATE_STEP = 6
+UPDATE_STEP = 8
 FILTER_STEP = 6
 LAST_STEP = 2
 VLIM = 56

time: 50.3 us -> 49.9 us (level)
    pallas_call x1, Pallas kernels: 46 us -> 45.5 us  [section(): pl.pallas_call(functools.partial(kernel, n, zn), out_shape=(OUT((5, X, Y,...]
where the time goes in v4:
time: 49.9 us; the launch traced here: 49.3 us
  Pallas kernels  48.7 us (98%)
  between operations  0.64 us (1%)
    pallas_call x1, Pallas kernels, section(): pl.pallas_call(functools.partial(kernel, n, zn), out_shape=(OUT((5, X, Y,...  45.5 us
    pallas_call x1, Pallas kernels, section(): pl.pallas_call(last_kernel, out_shape=(jax.ShapeDtypeStruct((5, X, Y, L),...  3.23 us

profile of v4, /device:TPU:0, one launch (start us, length us, event | category | flops | bytes accessed | tf_op | source)
XLA Modules:
  0.0 49.3 jit_solution(5817927722667294288)
XLA Ops:
  0.6 45.5 %shard_map.59 = (f32[5,24,64,128]{3,2,1,0:T(8,128)S(1)}, f32[5,24,64,128]{3,2,1,0:T(8,128)S(1)}, f32[80,8,128]{2,1,0:T(8,128)S(1)}) custom-call(f32[24,64,128]{2,1,0:T(8,128)} %rho_h.1, f32[3,24,64,128]{3,2,1,0:T(8,128)} %mom_h.1, f32[24,64,128]{2,1,0:T(8,128)} %en_h.1, f32[5,24,64,128]{3,2,1,0:T(8,128)} %inc_h.1), custom_call_target="tpu_custom_call" | custom-call | tf_op jit(solution)/shard_map/pallas_call | solution.py:588
  46.1 3.2 %shard_map.60 = (f32[5,24,64,128]{3,2,1,0:T(8,128)}, f32[5,24,64,128]{3,2,1,0:T(8,128)}) custom-call(f32[5,24,64,128]{3,2,1,0:T(8,128)S(1)} %get-tuple-element.5.z_ref, f32[5,24,64,128]{3,2,1,0:T(8,128)S(1)} %get-tuple-element.6.s_ref, f32[80,8,128]{2,1,0:T(8,128)S(1)} %get-tuple-element.7.carry_ref), custom_call_target="tpu_custom_call" | custom-call | tf_op jit(solution)/shard_map/pallas_call | solution.py:618
